TPU v7x, 32 devices: a whole 2x2x4 slice. The times are simulated.
32 devices in a mesh: layer: 4 (over y, core), row: 4 (over z), col: 2 (over x).
Axes of the slice: x: 2, y: 2, z: 4, core: 2. Of those that a mesh axis runs over, the one named last changes fastest.
Arguments:
- edge_weight: bfloat16 [2048, 2048], P('row', 'col'), may hold values from 0 to 1, as said below
Outputs:
- clustering: float32 [4, 512], P('row', ('layer', 'col'))
Inputs may be any that keep to these rules, and one draw needn't show every extreme that they name: `edge_weight`: symmetric with a zero diagonal; every vertex v is linked to v - 1 and v + 1 (modulo 2048); an edge's entry lies in [0.2, 1], all other entries are 0.
All inputs are finite; a program needn't handle non-finite values.
Results may differ from a plain program's by a relative error of at most 0.0003.
Values may be sent and summed in bfloat16 or wider, within the bound.
A program may use at most 64 MiB of HBM per device.

v0:
```python
import jax
import jax.numpy as jnp
from jax import lax
from jax.sharding import PartitionSpec as P

STRIPE = 128


def local(edge_weight):
    layers = lax.axis_size("layer")
    layer_index = lax.axis_index("layer")
    row_count, col_count = edge_weight.shape
    row_global = lax.axis_index("row") * row_count + jnp.arange(row_count, dtype=jnp.int32)
    col_global = lax.axis_index("col") * col_count + jnp.arange(col_count, dtype=jnp.int32)
    lower = jnp.where(
        row_global[:, None] > col_global[None, :], edge_weight, jnp.zeros_like(edge_weight)
    )
    column_groups = lower.reshape(row_count, col_count // (STRIPE * layers), layers, STRIPE)
    left_local = lax.dynamic_index_in_dim(column_groups, layer_index, 2, keepdims=False).reshape(
        row_count, col_count // layers
    )
    row_groups = lower.reshape(row_count // (STRIPE * layers), layers, STRIPE, col_count)
    right_local = lax.dynamic_index_in_dim(row_groups, layer_index, 1, keepdims=False).reshape(
        row_count // layers, col_count
    )
    left_whole = lax.all_gather(left_local, "col", axis=1, tiled=True)
    right_whole = lax.all_gather(right_local, "row", axis=0, tiled=True)
    paths = jnp.dot(left_whole, right_whole, preferred_element_type=jnp.float32)
    triangles = jnp.sum(paths * lower, axis=1)
    degree = jnp.sum(jnp.where(left_local > 0, 1.0, 0.0).astype(jnp.float32), axis=1)
    layer_share = (
        lax.psum_scatter(triangles, "layer", scatter_dimension=0, tiled=True),
        lax.psum_scatter(degree, "layer", scatter_dimension=0, tiled=True),
    )
    tri_total, degree_total = (
        lax.psum_scatter(layer_share[0], "col", scatter_dimension=0, tiled=True),
        lax.psum_scatter(layer_share[1], "col", scatter_dimension=0, tiled=True),
    )
    clustering = 2.0 * tri_total / jnp.maximum(degree_total * (degree_total - 1.0), 2.0)
    return clustering.reshape(1, -1)


def solution(mesh):
    placed = (P("row", "col"),)
    return jax.shard_map(
        local, mesh=mesh, in_specs=placed, out_specs=P("row", ("layer", "col")), check_vma=False
    )
```

profile of v0, /device:TPU:0, one launch (start us, length us, event | category | flops | bytes accessed | tf_op | source)
XLA Modules:
  0.0 60.3 jit_solution(14782072480402922622)
XLA Ops:
  6.5 0.0 all-gather.3.cloned.1.call-start
  6.5 1.5 %compare_select_fusion = bf16[512,1024]{1,0:T(8,128)(2,1)S(1)} fusion(bf16[512,1024]{1,0:T(8,128)(2,1)} %param.1, s32[1024]{0:T(1024)S(1)} %iota_add_fusion, s32[512]{0:T(512)S(1)} %iota_add_fusion.1), kind=kLoop, calls=%fused_computation.1 | loop fusion | flops 1048576 | bytes 2103296 | tf_op jit(solution)/shard_map/jit(_where)/select_n | solution.py:15
  8.1 0.7 %constant_dynamic-slice_fusion = bf16[1,1,128,1024]{3,2,1,0:T(8,128)(2,1)} fusion(bf16[1,4,128,1024]{3,2,1,0:T(8,128)(2,1)S(1)} %bitcast.10, s32[]{:T(128)S(6)} %select_n.16), kind=kLoop, calls=%fused_computation.10 | loop fusion | bytes 524292 | tf_op jit(solution)/shard_map/jit(dynamic_index_in_dim)/dynamic_slice | solution.py:23
  8.8 0.0 all-gather.3.cloned.1.call-update
  8.8 0.8 %reshape.25 = bf16[512,2,4,128]{3,2,1,0:T(4,128)(2,1)S(1)} reshape(bf16[512,1024]{1,0:T(8,128)(2,1)S(1)} %compare_select_fusion) | data formatting | bytes 2097152 | tf_op jit(solution)/shard_map/reshape | solution.py:18
  9.6 0.0 copy-start.1
  9.6 0.0 copy-start
  9.7 0.5 constant_dynamic-slice_fusion.1
  10.2 0.7 %copy.4 = bf16[512,2,1,128]{0,3,1,2:T(8,128)(2,1)S(1)} copy(bf16[512,2,1,128]{3,2,1,0:T(2,128)(2,1)S(1)} %constant_dynamic-slice_fusion.1) | data formatting | bytes 524288
  10.9 0.0 copy-done.1
  10.9 0.6 dynamic-slice
  11.5 0.0 copy-done
  11.5 0.6 %dynamic-slice.2 = u32[1]{0:T(128)} dynamic-slice(u32[32]{0:T(128)S(1)} %copy-done, u32[]{:T(128)S(6)} %add.41), dynamic_slice_sizes={1} | dynamic-slice | bytes 12
  13.4 9.9 %all_gather.6 = bf16[512,512]{0,1:T(8,128)(2,1)S(1)} all-gather(bf16[512,256]{0,1:T(8,128)(2,1)S(1)} %bitcast.11), channel_id=1, replica_groups=mesh['layer'=4,'row'=4,'col'=2] {'col'}, dimensions={1}, use_global_device_ids=true | all-gather | bytes 786432 | tf_op jit(solution)/shard_map/all_gather | solution.py:26
  23.3 0.1 select_reduce_fusion
  23.4 16.3 %all-gather.3.cloned.1.call-done = bf16[1,1,512,1024]{3,2,1,0:T(8,128)(2,1)} async-done(((bf16[1,1,128,1024]{3,2,1,0:T(8,128)(2,1)}), bf16[1,1,512,1024]{3,2,1,0:T(8,128)(2,1)}) %all-gather.3.cloned.1.call-update) | async-done | bytes 1048592 | tf_op jit(solution)/shard_map/all_gather | solution.py:27
  39.7 2.0 %multiply_reduce_fusion = f32[512]{0:T(512)S(1)} fusion(bf16[512,1024]{1,0:T(8,128)(2,1)S(1)} %compare_select_fusion, bf16[512,512]{0,1:T(8,128)(2,1)S(1)} %all_gather.6, bf16[1,1,512,1024]{3,2,1,0:T(8,128)(2,1)} %all-gather.3.cloned.1.call-done), kind=kOutput, calls=%fused_computation | convolution fusion | flops 538443264 | bytes 2623488 | tf_op jit(solution)/shard_map/dot_general | solution.py:28
  41.7 6.1 %all-reduce.4 = (f32[512]{0:T(512)S(1)}, f32[512]{0:T(512)S(1)}) all-reduce(f32[512]{0:T(512)S(1)} %select_reduce_fusion, f32[512]{0:T(512)S(1)} %multiply_reduce_fusion), channel_id=5, replica_groups=mesh['layer'=4,'row'=4,'col'=2] {'layer'}, use_global_device_ids=true, to_apply=%region_4.5.clone | all-reduce | flops 1024 | bytes 8192
  47.8 0.1 dynamic-slice.5
  47.9 0.1 dynamic-slice.1
  48.0 4.9 %all-reduce.5 = (f32[128]{0:T(128)S(1)}, f32[128]{0:T(128)S(1)}) all-reduce(f32[128]{0:T(128)S(1)} %dynamic-slice.5, f32[128]{0:T(128)S(1)} %dynamic-slice.1), channel_id=6, replica_groups=mesh['layer'=4,'row'=4,'col'=2] {'col'}, use_global_device_ids=true, to_apply=%region_5.6.clone | all-reduce | flops 256 | bytes 2048
  52.9 0.6 fusion.3
  (2 shorter events, 0.0 us)
Async XLA Ops:
  6.5 33.2 %all-gather.3.cloned.1.call-start = ((), (), s32[]{:S(2)}) async-start(), calls=%async_computation | async-start | bytes 1310720 | tf_op jit(solution)/shard_map/all_gather | solution.py:27
  9.6 1.3 %copy-start.1 = (u32[32]{0:T(128)S(1)}, u32[32]{0:T(128)}, u32[]{:S(2)}) copy-start(u32[32]{0:T(128)} %constant.39) | copy-start | bytes 388
  9.6 1.9 %copy-start = (u32[32]{0:T(128)S(1)}, u32[32]{0:T(128)}, u32[]{:S(2)}) copy-start(u32[32]{0:T(128)} %constant.43) | copy-start | bytes 388
Sparse Core Ops, SparseCore 0:
  9.0 30.6 all-gather.2
where the time goes:
time: 60.6 us; the launch traced here: 60.3 us
  blocking collectives  20.9 us (34%)
  waiting for transfers between devices  16.3 us (27%)
  between operations  14.7 us (24%)
  local copies, waits for them, and re-layouts  4.1 us (7%)
  other arithmetic  2.22 us (4%)
  matrix products  2.04 us (3%)
    all_gather x1, waiting for transfers between devices, local(): right_whole = lax.all_gather(right_local, 'row', axis=0, tiled=True)  16.3 us
    unnamed x2, blocking collectives  11 us
    all_gather x1, blocking collectives, local(): left_whole = lax.all_gather(left_local, 'col', axis=1, tiled=True)  9.94 us
    unnamed x9, local copies, waits for them, and re-layouts  2.05 us
    dot_general x1, matrix products, local(): paths = jnp.dot(left_whole, right_whole, preferred_element_type=jnp.float32)  2.04 us
    select_n x1, other arithmetic, local(): jnp.where(row_global[:, None] > col_global[None, :], edge_weight, jnp.zer...  1.53 us
  transfers between devices with their start and end apart: 1, of which 1 were waited for; matrix products, arithmetic and copies ran while one was open for 5% of the time, Pallas kernels for 0%

commit v1 on v0

--- a/solution.py
+++ b/solution.py
@@ -4,6 +4,22 @@
 from jax.sharding import PartitionSpec as P
 
 STRIPE = 128
+
+
+def apply_the_regions(local_x):
+    fan = lax.axis_size("row")
+    copies = tuple(((k0, (k0 + 1) % fan) for k0 in range(fan)))
+
+    def see_the_positions(work_now):
+        if len(work_now) == fan:
+            return work_now
+        r_now = see_the_positions([lax.ppermute(work_now[0], "row", copies), *work_now])
+        return r_now
+
+    frame_out = jnp.concatenate(see_the_positions([local_x]), axis=0)
+    piece_next = lax.axis_index("row")
+    far_arr = jnp.roll(frame_out, (piece_next + 1) * local_x.shape[0], axis=0)
+    return far_arr
 
 
 def local(edge_weight):
@@ -24,7 +40,7 @@
         row_count // layers, col_count
     )
     left_whole = lax.all_gather(left_local, "col", axis=1, tiled=True)
-    right_whole = lax.all_gather(right_local, "row", axis=0, tiled=True)
+    right_whole = apply_the_regions(right_local)
     paths = jnp.dot(left_whole, right_whole, preferred_element_type=jnp.float32)
     triangles = jnp.sum(paths * lower, axis=1)
     degree = jnp.sum(jnp.where(left_local > 0, 1.0, 0.0).astype(jnp.float32), axis=1)

time: 60.6 us -> 43.3 us (0.71)
  between operations: 14.7 us -> 1.5 us
  starting transfers between devices: 0.01 us -> 3.12 us
  blocking collectives: 20.9 us -> 17.8 us
  waiting for transfers between devices: 16.3 us -> 14 us
  matrix products: 2.04 us -> 0.82 us
    all_gather x1 -> x0, waiting for transfers between devices: 16.3 us -> none  [local(): right_whole = lax.all_gather(right_local, 'row', axis=0, tiled=True)]
    ppermute x0 -> x3, waiting for transfers between devices: none -> 14 us  [see_the_positions(): lax.ppermute(work_now[0], 'row', copies)]
    ppermute x0 -> x3, starting transfers between devices: none -> 3.12 us  [see_the_positions(): lax.ppermute(work_now[0], 'row', copies)]
    all_gather x1, blocking collectives: 9.94 us -> 7.27 us  [local(): left_whole = lax.all_gather(left_local, 'col', axis=1, tiled=True)]
    dot_general x1, matrix products: 2.04 us -> 0.82 us  [local(): paths = jnp.dot(left_whole, right_whole, preferred_element_type=jnp.float32)]
    dynamic_slice x1 -> x0, local copies, waits for them, and re-layouts: 0.74 us -> none  [local(): lax.dynamic_index_in_dim(row_groups, layer_index, 1, keepdims=False)]
    unnamed x9 -> x16, local copies, waits for them, and re-layouts: 2.05 us -> 2.23 us
  transfers between devices with their start and end apart: 1 -> 3, of which waited for: 1 -> 3; matrix products, arithmetic and copies ran while one was open for 5% -> 8% of each run, Pallas kernels for 0% -> 0%
where the time goes in v1:
time: 43.3 us; the launch traced here: 43.1 us
  blocking collectives  17.8 us (41%)
  waiting for transfers between devices  14 us (32%)
  local copies, waits for them, and re-layouts  3.58 us (8%)
  starting transfers between devices  3.12 us (7%)
  other arithmetic  2.22 us (5%)
  between operations  1.5 us (3%)
  matrix products  0.82 us (2%)
    ppermute x3, waiting for transfers between devices, see_the_positions(): lax.ppermute(work_now[0], 'row', copies)  14 us
    unnamed x2, blocking collectives  10.6 us
    all_gather x1, blocking collectives, local(): left_whole = lax.all_gather(left_local, 'col', axis=1, tiled=True)  7.27 us
    ppermute x3, starting transfers between devices, see_the_positions(): lax.ppermute(work_now[0], 'row', copies)  3.12 us
    unnamed x16, local copies, waits for them, and re-layouts  2.23 us
    select_n x1, other arithmetic, local(): jnp.where(row_global[:, None] > col_global[None, :], edge_weight, jnp.zer...  1.53 us
  transfers between devices with their start and end apart: 3, of which 3 were waited for; matrix products, arithmetic and copies ran while one was open for 8% of the time, Pallas kernels for 0%

profile of v1, /device:TPU:0, one launch (start us, length us, event | category | flops | bytes accessed | tf_op | source)
XLA Modules:
  0.0 43.1 jit_solution(4070823181122152081)
XLA Ops:
  0.0 1.5 %compare_select_fusion = bf16[512,1024]{1,0:T(8,128)(2,1)S(1)} fusion(bf16[512,1024]{1,0:T(8,128)(2,1)} %param.1, s32[1024]{0:T(1024)S(1)} %iota_add_fusion, s32[512]{0:T(512)S(1)} %iota_add_fusion.1), kind=kLoop, calls=%fused_computation.1 | loop fusion | flops 1048576 | bytes 2103296 | tf_op jit(solution)/shard_map/jit(_where)/select_n | solution.py:31
  1.6 0.0 copy-start.1
  1.6 0.0 copy-start
  1.6 3.1 %collective-permute-start = (bf16[128,1024]{1,0:T(8,128)(2,1)S(1)}, bf16[128,1024]{1,0:T(8,128)(2,1)S(1)}, u32[]{:S(2)}, u32[]{:S(2)}) collective-permute-start(bf16[128,1024]{1,0:T(8,128)(2,1)S(1)} %dynamic-slice_bitcast_fusion), channel_id=1, source_target_pairs={{0,2},{2,4},{4,6},{6,0},{1,3},{3,5},{5,7},{7,1},{8,10},{10,12},{12... | collective-permute-start | bytes 786440 | tf_op jit(solution)/shard_map/ppermute | solution.py:16
  4.7 8.3 %collective-permute-done = bf16[128,1024]{1,0:T(8,128)(2,1)S(1)} collective-permute-done((bf16[128,1024]{1,0:T(8,128)(2,1)S(1)}, bf16[128,1024]{1,0:T(8,128)(2,1)S(1)}, u32[]{:S(2)}, u32[]{:S(2)}) %collective-permute-start) | collective-permute-done | bytes 262176 | tf_op jit(solution)/shard_map/ppermute | solution.py:16
  13.0 0.0 collective-permute-start.1
  13.0 0.7 %reshape.25 = bf16[512,2,4,128]{3,2,1,0:T(4,128)(2,1)S(1)} reshape(bf16[512,1024]{1,0:T(8,128)(2,1)S(1)} %compare_select_fusion) | data formatting | bytes 2097152 | tf_op jit(solution)/shard_map/reshape | solution.py:34
  13.8 0.5 %constant_dynamic-slice_fusion = bf16[512,2,1,128]{3,2,1,0:T(2,128)(2,1)S(1)} fusion(bf16[512,2,4,128]{3,2,1,0:T(4,128)(2,1)S(1)} %reshape.25, s32[]{:T(128)S(6)} %select_n.29), kind=kLoop, calls=%fused_computation.17 | loop fusion | bytes 524292 | tf_op jit(solution)/shard_map/jit(dynamic_index_in_dim)/dynamic_slice | solution.py:35
  14.4 0.7 %copy.4 = bf16[512,2,1,128]{0,3,1,2:T(8,128)(2,1)S(1)} copy(bf16[512,2,1,128]{3,2,1,0:T(2,128)(2,1)S(1)} %constant_dynamic-slice_fusion) | data formatting | bytes 524288
  15.1 0.0 copy-done.1
  15.1 0.6 %dynamic-slice = u32[1]{0:T(128)} dynamic-slice(u32[32]{0:T(128)S(1)} %copy-done.1, u32[]{:T(128)S(6)} %add.57), dynamic_slice_sizes={1} | dynamic-slice | bytes 12
  15.7 0.0 copy-done
  15.7 0.7 %dynamic-slice.2 = u32[1]{0:T(128)} dynamic-slice(u32[32]{0:T(128)S(1)} %copy-done, u32[]{:T(128)S(6)} %add.57), dynamic_slice_sizes={1} | dynamic-slice | bytes 12
  17.7 4.6 %collective-permute-done.1 = bf16[128,1024]{1,0:T(8,128)(2,1)S(1)} collective-permute-done((bf16[128,1024]{1,0:T(8,128)(2,1)S(1)}, bf16[128,1024]{1,0:T(8,128)(2,1)S(1)}, u32[]{:S(2)}, u32[]{:S(2)}) %collective-permute-start.1) | collective-permute-done | bytes 262176 | tf_op jit(solution)/shard_map/ppermute | solution.py:16
  22.3 0.0 collective-permute-start.2
  22.3 7.3 %all_gather.3 = bf16[512,512]{0,1:T(8,128)(2,1)S(1)} all-gather(bf16[512,256]{0,1:T(8,128)(2,1)S(1)} %bitcast.16), channel_id=1, replica_groups=mesh['layer'=4,'row'=4,'col'=2] {'col'}, dimensions={1}, use_global_device_ids=true | all-gather | bytes 786432 | tf_op jit(solution)/shard_map/all_gather | solution.py:42
  29.6 0.1 select_reduce_fusion
  29.7 1.0 %collective-permute-done.2 = bf16[128,1024]{1,0:T(8,128)(2,1)S(1)} collective-permute-done((bf16[128,1024]{1,0:T(8,128)(2,1)S(1)}, bf16[128,1024]{1,0:T(8,128)(2,1)S(1)}, u32[]{:S(2)}, u32[]{:S(2)}) %collective-permute-start.2) | collective-permute-done | bytes 262176 | tf_op jit(solution)/shard_map/ppermute | solution.py:16
  31.0 0.8 %multiply_reduce_fusion = f32[512]{0:T(512)S(1)} fusion(bf16[512,1024]{1,0:T(8,128)(2,1)S(1)} %compare_select_fusion, bf16[512,512]{0,1:T(8,128)(2,1)S(1)} %all_gather.3, bf16[1024,1024]{1,0:T(8,128)(2,1)S(1)} %constant_dynamic-update-slice_fusion, s32[]{:T(128)S(6)} %select_n.31), kind=kOutput, calls=%fused_computation | convolution fusion | flops 538443264 | bytes 2623492 | tf_op jit(solution)/shard_map/dot_general | solution.py:44
  31.8 5.7 %all-reduce.4 = (f32[512]{0:T(512)S(1)}, f32[512]{0:T(512)S(1)}) all-reduce(f32[512]{0:T(512)S(1)} %select_reduce_fusion, f32[512]{0:T(512)S(1)} %multiply_reduce_fusion), channel_id=4, replica_groups=mesh['layer'=4,'row'=4,'col'=2] {'layer'}, use_global_device_ids=true, to_apply=%region_4.5.clone | all-reduce | flops 1024 | bytes 8192
  37.4 0.1 dynamic-slice.1
  37.5 0.1 dynamic-slice.5
  37.6 4.9 %all-reduce.5 = (f32[128]{0:T(128)S(1)}, f32[128]{0:T(128)S(1)}) all-reduce(f32[128]{0:T(128)S(1)} %dynamic-slice.5, f32[128]{0:T(128)S(1)} %dynamic-slice.1), channel_id=5, replica_groups=mesh['layer'=4,'row'=4,'col'=2] {'col'}, use_global_device_ids=true, to_apply=%region_5.6.clone | all-reduce | flops 256 | bytes 2048
  42.5 0.6 %fusion.4 = f32[1,64]{1,0:T(1,128)} fusion(f32[128]{0:T(128)S(1)} %get-tuple-element.7, u32[]{:T(128)S(6)} %multiply.3, f32[128]{0:T(128)S(1)} %get-tuple-element.8), kind=kLoop, calls=%fused_computation.21 | loop fusion | flops 320 | bytes 772 | tf_op jit(solution)/shard_map/reshape | solution.py:56
  (11 shorter events, 0.2 us)
Async XLA Ops:
  1.6 13.5 %copy-start.1 = (u32[32]{0:T(128)S(1)}, u32[32]{0:T(128)}, u32[]{:S(2)}) copy-start(u32[32]{0:T(128)} %constant.63) | copy-start | bytes 388
  1.6 14.1 %copy-start = (u32[32]{0:T(128)S(1)}, u32[32]{0:T(128)}, u32[]{:S(2)}) copy-start(u32[32]{0:T(128)} %constant.67) | copy-start | bytes 388
  1.6 11.4 %collective-permute-start = (bf16[128,1024]{1,0:T(8,128)(2,1)S(1)}, bf16[128,1024]{1,0:T(8,128)(2,1)S(1)}, u32[]{:S(2)}, u32[]{:S(2)}) collective-permute-start(bf16[128,1024]{1,0:T(8,128)(2,1)S(1)} %dynamic-slice_bitcast_fusion), channel_id=1, source_target_pairs={{0,2},{2,4},{4,6},{6,0},{1,3},{3,5},{5,7},{7,1},{8,10},{10,12},{12... | collective-permute-start | bytes 786440 | tf_op jit(solution)/shard_map/ppermute | solution.py:16
  13.0 9.3 %collective-permute-start.1 = (bf16[128,1024]{1,0:T(8,128)(2,1)S(1)}, bf16[128,1024]{1,0:T(8,128)(2,1)S(1)}, u32[]{:S(2)}, u32[]{:S(2)}) collective-permute-start(bf16[128,1024]{1,0:T(8,128)(2,1)S(1)} %collective-permute-done), channel_id=1, source_target_pairs={{0,2},{2,4},{4,6},{6,0},{1,3},{3,5},{5,7},{7,1},{8,10},{10,12},{12... | collective-permute-start | bytes 786440 | tf_op jit(solution)/shard_map/ppermute | solution.py:16
  22.3 8.4 %collective-permute-start.2 = (bf16[128,1024]{1,0:T(8,128)(2,1)S(1)}, bf16[128,1024]{1,0:T(8,128)(2,1)S(1)}, u32[]{:S(2)}, u32[]{:S(2)}) collective-permute-start(bf16[128,1024]{1,0:T(8,128)(2,1)S(1)} %collective-permute-done.1), channel_id=1, source_target_pairs={{0,2},{2,4},{4,6},{6,0},{1,3},{3,5},{5,7},{7,1},{8,10},{10,12},{12... | collective-permute-start | bytes 786440 | tf_op jit(solution)/shard_map/ppermute | solution.py:16
